TPU v7x, 32 devices: a whole 2x2x4 slice. The times are simulated.
32 devices in a mesh: row: 4 (over y, x), col: 8 (over z, core).
Axes of the slice: x: 2, y: 2, z: 4, core: 2. Of those that a mesh axis runs over, the one named last changes fastest.
Arguments:
- trailing: float32 [3072, 3072], P('row', 'col'), may hold values from -6 to 6, as said below
- v_panels: bfloat16 [3, 3072, 256], P(None, ('row', 'col')), may hold values from -6 to 6
Outputs:
- updated: float32 [3072, 3072], P('row', 'col')
- w_panels: float32 [3, 3072, 256], P(None, ('row', 'col'))
Inputs may be any that keep to these rules, and one draw needn't show every extreme that they name: trailing is symmetric: entry (i, j) equals entry (j, i).
All inputs are finite; a program needn't handle non-finite values.
Results may differ from a plain program's by a relative error of at most 0.0003.
Values may be sent and summed in bfloat16 or wider, within the bound.
A program may use at most 64 MiB of HBM per device.

v0:
```python
import math
import jax
import jax.numpy as jnp
from jax import lax
from jax.sharding import PartitionSpec as P


def broadcast(value, axis, root):
    mine = lax.axis_index(axis) == root
    return lax.psum(jnp.where(mine, value, jnp.zeros_like(value)), axis)


def on_device(trailing, v_panels):
    rows_tile = trailing.shape[0]
    cols_tile = trailing.shape[1]
    count_row = lax.axis_size("row")
    full_order = rows_tile * count_row
    scaling = 1.0 / math.sqrt(full_order)
    group_ratio = rows_tile // cols_tile
    col_index = lax.axis_index("col")
    root_row = col_index // group_ratio
    offset = col_index % group_ratio * cols_tile
    ticks_all = v_panels.shape[0]
    highest = lax.Precision.HIGHEST
    v_rows_all = lax.all_gather(v_panels, "col", axis=1, tiled=True)
    v_mirror_all = broadcast(v_rows_all, "row", root_row)
    v_cols_all = lax.dynamic_slice_in_dim(v_mirror_all, offset, cols_tile, 1)
    current = trailing
    w_list = []
    for tick in range(ticks_all):
        v_rows = v_rows_all[tick]
        v_cols = v_cols_all[tick]
        v_rows_f = v_rows.astype(jnp.float32)
        v_cols_f = v_cols.astype(jnp.float32)
        block = current
        summed = lax.psum_scatter(
            jnp.dot(block, v_cols_f, precision=highest, preferred_element_type=jnp.float32),
            "col",
            scatter_dimension=0,
            tiled=True,
        )
        w_piece = summed * scaling
        w_rows = lax.all_gather(w_piece, "col", axis=0, tiled=True)
        w_mirror = broadcast(w_rows, "row", root_row)
        w_cols = lax.dynamic_slice_in_dim(w_mirror, offset, cols_tile, 0)
        rows_side = jnp.concatenate([v_rows_f, w_rows], axis=1)
        cols_side = jnp.concatenate([w_cols, v_cols_f], axis=1)
        update = lax.dot_general(
            rows_side,
            cols_side,
            (((1,), (1,)), ((), ())),
            precision=highest,
            preferred_element_type=jnp.float32,
        )
        current = current - update * (0.5 * scaling)
        w_list.append(w_piece)
    return (current, jnp.stack(w_list, axis=0))


def solution(mesh):
    in_specs = (P("row", "col"), P(None, ("row", "col"), None))
    out_specs = (P("row", "col"), P(None, ("row", "col"), None))
    return jax.shard_map(
        on_device, mesh=mesh, in_specs=in_specs, out_specs=out_specs, check_vma=False
    )
```

profile of v0, /device:TPU:0, one launch (start us, length us, event | category | flops | bytes accessed | tf_op | source)
XLA Modules:
  0.0 415.8 jit_solution(6455830931447291190)
XLA Ops:
  8.0 27.2 %all-gather.2.cloned.1.call-done = bf16[3,768,256]{2,1,0:T(8,128)(2,1)} async-done(((bf16[3,96,256]{2,1,0:T(8,128)(2,1)}), bf16[3,768,256]{2,1,0:T(8,128)(2,1)}) %all-gather.2.cloned.1.call-update) | async-done | bytes 1179664 | tf_op jit(solution)/shard_map/all_gather | solution.py:25
  35.1 2.4 broadcast_select_fusion
  37.6 55.3 %all-reduce.5.cloned.1.call-done = bf16[3,768,256]{2,1,0:T(8,128)(2,1)} async-done(((bf16[3,768,256]{2,1,0:T(8,128)(2,1)}), bf16[3,768,256]{2,1,0:T(8,128)(2,1)}) %all-reduce.5.cloned.1.call-update) | async-done | bytes 1179664 | tf_op jit(solution)/shard_map/psum | solution.py:10
  92.8 1.8 convolution_bitcast_fusion
  94.7 1.1 copy.16
  95.9 31.9 %reduce-scatter.10.cloned.1.call-done = f32[96,256]{1,0:T(8,128)} async-done(((f32[768,256]{1,0:T(8,128)}), f32[96,256]{1,0:T(8,128)}) %reduce-scatter.10.cloned.1.call-update) | async-done | bytes 98320
  127.9 1.0 copy.17
  129.6 15.7 %all_gather.13 = f32[768,256]{1,0:T(8,128)S(1)} all-gather(f32[96,256]{1,0:T(8,128)S(1)} %copy.8), channel_id=1, replica_groups=mesh['row'=4,'col'=8] {'col'}, dimensions={0}, use_global_device_ids=true | all-gather | bytes 884736 | tf_op jit(solution)/shard_map/all_gather | solution.py:43
  145.4 1.0 broadcast_select_fusion.3
  146.9 1.4 fusion.39
  148.9 1.0 fusion.45
  149.9 43.8 %all-reduce.7.cloned.1.call-done = f32[768,256]{1,0:T(8,128)} async-done(((f32[768,256]{1,0:T(8,128)}), f32[768,256]{1,0:T(8,128)}) %all-reduce.7.cloned.1.call-update) | async-done | bytes 786448 | tf_op jit(solution)/shard_map/psum | solution.py:10
  193.6 1.1 constant_dynamic-slice_fusion.2
  194.9 3.6 fusion.27
  198.5 2.6 fusion.44
  201.2 31.9 %reduce-scatter.12.cloned.1.call-done = f32[96,256]{1,0:T(8,128)} async-done(((f32[768,256]{1,0:T(8,128)}), f32[96,256]{1,0:T(8,128)}) %reduce-scatter.12.cloned.1.call-update) | async-done | bytes 98320
  233.1 1.0 copy.19
  234.9 15.7 %all_gather.14 = f32[768,256]{1,0:T(8,128)S(1)} all-gather(f32[96,256]{1,0:T(8,128)S(1)} %copy.10), channel_id=1, replica_groups=mesh['row'=4,'col'=8] {'col'}, dimensions={0}, use_global_device_ids=true | all-gather | bytes 884736 | tf_op jit(solution)/shard_map/all_gather | solution.py:43
  250.6 0.9 broadcast_select_fusion.2
  251.6 47.2 %all-reduce.9.cloned.1.call-done = f32[768,256]{1,0:T(8,128)} async-done(((f32[768,256]{1,0:T(8,128)}), f32[768,256]{1,0:T(8,128)}) %all-reduce.9.cloned.1.call-update) | async-done | bytes 786448 | tf_op jit(solution)/shard_map/psum | solution.py:10
  298.8 1.0 constant_dynamic-slice_fusion.1
  299.8 3.9 fusion.21
  303.7 2.6 fusion.46
  306.4 31.9 %reduce-scatter.14.cloned.1.call-done = f32[96,256]{1,0:T(8,128)} async-done(((f32[768,256]{1,0:T(8,128)}), f32[96,256]{1,0:T(8,128)}) %reduce-scatter.14.cloned.1.call-update) | async-done | bytes 98320
  338.3 1.0 copy.21
  340.1 15.9 %all_gather.15 = f32[768,256]{1,0:T(8,128)S(1)} all-gather(f32[96,256]{1,0:T(8,128)S(1)} %copy.12), channel_id=1, replica_groups=mesh['row'=4,'col'=8] {'col'}, dimensions={0}, use_global_device_ids=true | all-gather | bytes 884736 | tf_op jit(solution)/shard_map/all_gather | solution.py:43
  356.0 1.0 broadcast_select_fusion.1
  357.0 1.1 pad_maximum_fusion
  358.1 0.9 copy.13
  359.0 45.2 %all-reduce.11.cloned.1.call-done = f32[768,256]{1,0:T(8,128)} async-done(((f32[768,256]{1,0:T(8,128)}), f32[768,256]{1,0:T(8,128)}) %all-reduce.11.cloned.1.call-update) | async-done | bytes 786448 | tf_op jit(solution)/shard_map/psum | solution.py:10
  404.3 1.0 constant_dynamic-slice_fusion
  405.3 3.6 fusion.15
  (32 shorter events, 4.6 us)
Async XLA Ops:
  7.2 28.0 %all-gather.2.cloned.1.call-start = ((), (), s32[]{:S(2)}) async-start(), calls=%async_computation.3 | async-start | bytes 1327104 | tf_op jit(solution)/shard_map/all_gather | solution.py:25
  7.9 84.9 %all-reduce.5.cloned.1.call-start = ((), (), s32[]{:S(2)}) async-start(), calls=%async_computation.4 | async-start | bytes 2359296 | tf_op jit(solution)/shard_map/psum | solution.py:10
  37.5 55.4 %copy-start.1 = (f32[768,384]{1,0:T(8,128)S(1)}, f32[768,384]{1,0:T(8,128)}, u32[]{:S(2)}) copy-start(f32[768,384]{1,0:T(8,128)} %param.2) | copy-start | bytes 3538948
  37.5 90.3 %reduce-scatter.10.cloned.1.call-start = ((), (), s32[]{:S(2)}) async-start(), calls=%async_computation.8 | async-start | bytes 884736
  95.9 97.8 %all-reduce.7.cloned.1.call-start = ((), (), s32[]{:S(2)}) async-start(), calls=%async_computation.5 | async-start | bytes 1572864 | tf_op jit(solution)/shard_map/psum | solution.py:10
  145.3 1.6 copy-start
  146.3 86.8 %reduce-scatter.12.cloned.1.call-start = ((), (), s32[]{:S(2)}) async-start(), calls=%async_computation.9 | async-start | bytes 884736
  146.9 2.0 copy-start.4
  193.6 1.3 copy-start.3
  201.1 97.7 %all-reduce.9.cloned.1.call-start = ((), (), s32[]{:S(2)}) async-start(), calls=%async_computation.6 | async-start | bytes 1572864 | tf_op jit(solution)/shard_map/psum | solution.py:10
  251.6 86.8 %reduce-scatter.14.cloned.1.call-start = ((), (), s32[]{:S(2)}) async-start(), calls=%async_computation.10 | async-start | bytes 884736
  306.3 97.9 %all-reduce.11.cloned.1.call-start = ((), (), s32[]{:S(2)}) async-start(), calls=%async_computation.7 | async-start | bytes 1572864 | tf_op jit(solution)/shard_map/psum | solution.py:10
  357.0 48.3 %copy-start.2 = (f32[768,256]{1,0:T(8,128)S(1)}, f32[768,256]{1,0:T(8,128)}, u32[]{:S(2)}) copy-start(f32[768,256]{1,0:T(8,128)} %get-tuple-element.9) | copy-start | bytes 2359300
Sparse Core Ops, SparseCore 0:
  9.6 25.4 all-gather.1
  38.8 53.9 all-reduce.4
  96.0 31.8 reduce-scatter.9
  146.5 47.1 all-reduce.6
  201.2 31.8 reduce-scatter.11
  251.7 47.1 all-reduce.8
  306.5 31.8 reduce-scatter.13
  357.1 47.1 all-reduce.10
where the time goes:
time: 416 us
  waiting for transfers between devices  315 us (76%)
  blocking collectives  47.4 us (11%)
  matrix products  18.1 us (4%)
  between operations  14.3 us (3%)
  other arithmetic  10.8 us (3%)
  local copies, waits for them, and re-layouts  9.55 us (2%)
    psum x4, waiting for transfers between devices, broadcast(): return lax.psum(jnp.where(mine, value, jnp.zeros_like(value)), axis)  192 us
    unnamed x11, waiting for transfers between devices  96.6 us
    all_gather x3, blocking collectives, on_device(): w_rows = lax.all_gather(w_piece, 'col', axis=0, tiled=True)  47.4 us
    all_gather x1, waiting for transfers between devices, on_device(): v_rows_all = lax.all_gather(v_panels, 'col', axis=1, tiled=True)  27.2 us
    dot_general x3, matrix products, on_device(): lax.dot_general(rows_side, cols_side, (((1,), (1,)), ((), ())), precision...  11.1 us
  transfers between devices with their start and end apart: 8, of which 8 were waited for; matrix products, arithmetic and copies ran while one was open for 1% of the time, Pallas kernels for 0%

commit v1 on v0

--- a/solution.py
+++ b/solution.py
@@ -40,7 +40,25 @@
             tiled=True,
         )
         w_piece = summed * scaling
-        w_rows = lax.all_gather(w_piece, "col", axis=0, tiled=True)
+        size, index, span = (lax.axis_size("col"), lax.axis_index("col"), w_piece.shape[0])
+        forward = [(i, (i + 1) % size) for i in range(size)]
+        left = [(i, (i - 1) % size) for i in range(size)]
+        w_rows = jnp.zeros(
+            (*w_piece.shape[:0], size * span, *w_piece.shape[0 + 1 :]), w_piece.dtype
+        )
+        w_rows = lax.dynamic_update_slice_in_dim(w_rows, w_piece, index * span, axis=0)
+        from_left = from_right = w_piece
+        middle = size // 2
+        for step in range(1, middle + 1):
+            from_left = lax.ppermute(from_left, "col", forward)
+            w_rows = lax.dynamic_update_slice_in_dim(
+                w_rows, from_left, (index - step) % size * span, axis=0
+            )
+            if step < size - middle:
+                from_right = lax.ppermute(from_right, "col", left)
+                w_rows = lax.dynamic_update_slice_in_dim(
+                    w_rows, from_right, (index + step) % size * span, axis=0
+                )
         w_mirror = broadcast(w_rows, "row", root_row)
         w_cols = lax.dynamic_slice_in_dim(w_mirror, offset, cols_tile, 0)
         rows_side = jnp.concatenate([v_rows_f, w_rows], axis=1)

time: 416 us -> 446 us (1.072)
  blocking collectives: 47.4 us -> 0 us
  waiting for transfers between devices: 315 us -> 356 us
  starting transfers between devices: 0.33 us -> 33.2 us
    all_gather x3 -> x0, blocking collectives: 47.4 us -> none  [on_device(): w_rows = lax.all_gather(w_piece, 'col', axis=0, tiled=True)]
    ppermute x0 -> x21, waiting for transfers between devices: none -> 41.6 us  [the longest x12 41.6 us: on_device(): from_left = lax.ppermute(from_left, 'col', forward)]
    ppermute x0 -> x21, starting transfers between devices: none -> 32.7 us  [the longest x9 32 us: on_device(): from_right = lax.ppermute(from_right, 'col', left)]
  transfers between devices with their start and end apart: 8 -> 29, of which waited for: 8 -> 20; matrix products, arithmetic and copies ran while one was open for 1% -> 1% of each run, Pallas kernels for 0% -> 0%
where the time goes in v1:
time: 446 us; the launch traced here: 445 us
  waiting for transfers between devices  356 us (80%)
  starting transfers between devices  33.2 us (7%)
  matrix products  18.1 us (4%)
  between operations  14.9 us (3%)
  local copies, waits for them, and re-layouts  11.8 us (3%)
  other arithmetic  10.9 us (2%)
    psum x4, waiting for transfers between devices, broadcast(): return lax.psum(jnp.where(mine, value, jnp.zeros_like(value)), axis)  191 us
    unnamed x11, waiting for transfers between devices  96.5 us
    ppermute x12, waiting for transfers between devices, on_device(): from_left = lax.ppermute(from_left, 'col', forward)  41.6 us
    ppermute x9, starting transfers between devices, on_device(): from_right = lax.ppermute(from_right, 'col', left)  32 us
    all_gather x1, waiting for transfers between devices, on_device(): v_rows_all = lax.all_gather(v_panels, 'col', axis=1, tiled=True)  27.2 us
    dot_general x3, matrix products, on_device(): lax.dot_general(rows_side, cols_side, (((1,), (1,)), ((), ())), precision...  11.1 us
  transfers between devices with their start and end apart: 29, of which 20 were waited for; matrix products, arithmetic and copies ran while one was open for 1% of the time, Pallas kernels for 0%

profile of v1, /device:TPU:0, one launch (start us, length us, event | category | flops | bytes accessed | tf_op | source)
XLA Modules:
  0.0 445.2 jit_solution(2246876678098563205)
XLA Ops:
  8.0 27.2 %all-gather.2.cloned.1.call-done = bf16[3,768,256]{2,1,0:T(8,128)(2,1)} async-done(((bf16[3,96,256]{2,1,0:T(8,128)(2,1)}), bf16[3,768,256]{2,1,0:T(8,128)(2,1)}) %all-gather.2.cloned.1.call-update) | async-done | bytes 1179664 | tf_op jit(solution)/shard_map/all_gather | solution.py:25
  37.6 55.3 %all-reduce.5.cloned.1.call-done = bf16[3,768,256]{2,1,0:T(8,128)(2,1)} async-done(((bf16[3,768,256]{2,1,0:T(8,128)(2,1)}), bf16[3,768,256]{2,1,0:T(8,128)(2,1)}) %all-reduce.5.cloned.1.call-update) | async-done | bytes 1179664 | tf_op jit(solution)/shard_map/psum | solution.py:10
  96.0 31.8 %reduce-scatter.10.cloned.1.call-done = f32[96,256]{1,0:T(8,128)} async-done(((f32[768,256]{1,0:T(8,128)}), f32[96,256]{1,0:T(8,128)}) %reduce-scatter.10.cloned.1.call-update) | async-done | bytes 98320
  129.7 3.5 collective-permute-start.1
  133.3 2.7 collective-permute-done
  136.3 3.6 collective-permute-start.3
  139.9 2.7 collective-permute-done.2
  142.8 3.6 collective-permute-start.5
  146.4 2.5 collective-permute-done.4
  149.2 6.0 %collective-permute-done.6 = f32[96,256]{0,1:T(8,128)S(1)} collective-permute-done((f32[96,256]{0,1:T(8,128)S(1)}, f32[96,256]{0,1:T(8,128)S(1)}, u32[]{:S(2)}, u32[]{:S(2)}) %collective-permute-start.6) | collective-permute-done | bytes 98336 | tf_op jit(solution)/shard_map/ppermute | solution.py:53
  159.8 43.7 %all-reduce.7.cloned.1.call-done = f32[768,256]{1,0:T(8,128)} async-done(((f32[768,256]{1,0:T(8,128)}), f32[768,256]{1,0:T(8,128)}) %all-reduce.7.cloned.1.call-update) | async-done | bytes 786448 | tf_op jit(solution)/shard_map/psum | solution.py:10
  204.7 3.6 fusion.27
  208.4 2.6 fusion.44
  211.0 31.9 %reduce-scatter.12.cloned.1.call-done = f32[96,256]{1,0:T(8,128)} async-done(((f32[768,256]{1,0:T(8,128)}), f32[96,256]{1,0:T(8,128)}) %reduce-scatter.12.cloned.1.call-update) | async-done | bytes 98320
  244.8 3.5 collective-permute-start.8
  248.4 2.7 collective-permute-done.7
  251.4 3.6 collective-permute-start.10
  255.0 2.7 collective-permute-done.9
  257.9 3.6 collective-permute-start.12
  264.3 6.0 %collective-permute-done.13 = f32[96,256]{0,1:T(8,128)S(1)} collective-permute-done((f32[96,256]{0,1:T(8,128)S(1)}, f32[96,256]{0,1:T(8,128)S(1)}, u32[]{:S(2)}, u32[]{:S(2)}) %collective-permute-start.13) | collective-permute-done | bytes 98336 | tf_op jit(solution)/shard_map/ppermute | solution.py:53
  271.6 46.9 %all-reduce.9.cloned.1.call-done = f32[768,256]{1,0:T(8,128)} async-done(((f32[768,256]{1,0:T(8,128)}), f32[768,256]{1,0:T(8,128)}) %all-reduce.9.cloned.1.call-update) | async-done | bytes 786448 | tf_op jit(solution)/shard_map/psum | solution.py:10
  319.6 3.9 fusion.21
  323.4 2.6 fusion.46
  326.1 31.9 %reduce-scatter.14.cloned.1.call-done = f32[96,256]{1,0:T(8,128)} async-done(((f32[768,256]{1,0:T(8,128)}), f32[96,256]{1,0:T(8,128)}) %reduce-scatter.14.cloned.1.call-update) | async-done | bytes 98320
  359.9 3.5 collective-permute-start.15
  363.5 2.7 collective-permute-done.14
  366.5 3.6 collective-permute-start.17
  370.1 2.7 collective-permute-done.16
  373.0 3.6 collective-permute-start.19
  379.4 6.0 %collective-permute-done.20 = f32[96,256]{0,1:T(8,128)S(1)} collective-permute-done((f32[96,256]{0,1:T(8,128)S(1)}, f32[96,256]{0,1:T(8,128)S(1)}, u32[]{:S(2)}, u32[]{:S(2)}) %collective-permute-start.20) | collective-permute-done | bytes 98336 | tf_op jit(solution)/shard_map/ppermute | solution.py:53
  388.5 45.1 %all-reduce.11.cloned.1.call-done = f32[768,256]{1,0:T(8,128)} async-done(((f32[768,256]{1,0:T(8,128)}), f32[768,256]{1,0:T(8,128)}) %all-reduce.11.cloned.1.call-update) | async-done | bytes 786448 | tf_op jit(solution)/shard_map/psum | solution.py:10
  434.7 3.6 fusion.15
  (119 shorter events, 31.5 us)
Async XLA Ops:
  7.2 28.0 %all-gather.2.cloned.1.call-start = ((), (), s32[]{:S(2)}) async-start(), calls=%async_computation.3 | async-start | bytes 1327104 | tf_op jit(solution)/shard_map/all_gather | solution.py:25
  7.9 84.9 %all-reduce.5.cloned.1.call-start = ((), (), s32[]{:S(2)}) async-start(), calls=%async_computation.4 | async-start | bytes 2359296 | tf_op jit(solution)/shard_map/psum | solution.py:10
  37.5 55.4 %copy-start.1 = (f32[768,384]{1,0:T(8,128)S(1)}, f32[768,384]{1,0:T(8,128)}, u32[]{:S(2)}) copy-start(f32[768,384]{1,0:T(8,128)} %param.2) | copy-start | bytes 3538948
  37.5 90.3 %reduce-scatter.10.cloned.1.call-start = ((), (), s32[]{:S(2)}) async-start(), calls=%async_computation.8 | async-start | bytes 884736
  95.9 107.6 %all-reduce.7.cloned.1.call-start = ((), (), s32[]{:S(2)}) async-start(), calls=%async_computation.5 | async-start | bytes 1572864 | tf_op jit(solution)/shard_map/psum | solution.py:10
  129.6 6.4 %collective-permute-start = (f32[96,256]{0,1:T(8,128)S(1)}, f32[96,256]{0,1:T(8,128)S(1)}, u32[]{:S(2)}, u32[]{:S(2)}) collective-permute-start(f32[96,256]{0,1:T(8,128)S(1)} %get-tuple-element.13), channel_id=1, source_target_pairs={{0,1},{1,2},{2,3},{3,4},{4,5},{5,6},{6,7},{7,0},{8,9},{9,10},{10,1... | collective-permute-start | bytes 294920 | tf_op jit(solution)/shard_map/ppermute | solution.py:53
  129.7 6.5 %collective-permute-start.1 = (f32[96,256]{0,1:T(8,128)S(1)}, f32[96,256]{0,1:T(8,128)S(1)}, u32[]{:S(2)}, u32[]{:S(2)}) collective-permute-start(f32[96,256]{0,1:T(8,128)S(1)} %get-tuple-element.13), channel_id=1, source_target_pairs={{0,7},{1,0},{2,1},{3,2},{4,3},{5,4},{6,5},{7,6},{8,15},{9,8},{10,9... | collective-permute-start | bytes 294920 | tf_op jit(solution)/shard_map/ppermute | solution.py:58
  136.1 6.4 %collective-permute-start.2 = (f32[96,256]{0,1:T(8,128)S(1)}, f32[96,256]{0,1:T(8,128)S(1)}, u32[]{:S(2)}, u32[]{:S(2)}) collective-permute-start(f32[96,256]{0,1:T(8,128)S(1)} %collective-permute-done), channel_id=1, source_target_pairs={{0,1},{1,2},{2,3},{3,4},{4,5},{5,6},{6,7},{7,0},{8,9},{9,10},{10,1... | collective-permute-start | bytes 294920 | tf_op jit(solution)/shard_map/ppermute | solution.py:53
  136.3 6.4 %collective-permute-start.3 = (f32[96,256]{0,1:T(8,128)S(1)}, f32[96,256]{0,1:T(8,128)S(1)}, u32[]{:S(2)}, u32[]{:S(2)}) collective-permute-start(f32[96,256]{0,1:T(8,128)S(1)} %collective-permute-done.1), channel_id=1, source_target_pairs={{0,7},{1,0},{2,1},{3,2},{4,3},{5,4},{6,5},{7,6},{8,15},{9,8},{10,9... | collective-permute-start | bytes 294920 | tf_op jit(solution)/shard_map/ppermute | solution.py:58
  142.6 6.2 %collective-permute-start.4 = (f32[96,256]{0,1:T(8,128)S(1)}, f32[96,256]{0,1:T(8,128)S(1)}, u32[]{:S(2)}, u32[]{:S(2)}) collective-permute-start(f32[96,256]{0,1:T(8,128)S(1)} %collective-permute-done.2), channel_id=1, source_target_pairs={{0,1},{1,2},{2,3},{3,4},{4,5},{5,6},{6,7},{7,0},{8,9},{9,10},{10,1... | collective-permute-start | bytes 294920 | tf_op jit(solution)/shard_map/ppermute | solution.py:53
  142.8 6.2 %collective-permute-start.5 = (f32[96,256]{0,1:T(8,128)S(1)}, f32[96,256]{0,1:T(8,128)S(1)}, u32[]{:S(2)}, u32[]{:S(2)}) collective-permute-start(f32[96,256]{0,1:T(8,128)S(1)} %collective-permute-done.3), channel_id=1, source_target_pairs={{0,7},{1,0},{2,1},{3,2},{4,3},{5,4},{6,5},{7,6},{8,15},{9,8},{10,9... | collective-permute-start | bytes 294920 | tf_op jit(solution)/shard_map/ppermute | solution.py:58
  149.0 6.2 %collective-permute-start.6 = (f32[96,256]{0,1:T(8,128)S(1)}, f32[96,256]{0,1:T(8,128)S(1)}, u32[]{:S(2)}, u32[]{:S(2)}) collective-permute-start(f32[96,256]{0,1:T(8,128)S(1)} %collective-permute-done.4), channel_id=1, source_target_pairs={{0,1},{1,2},{2,3},{3,4},{4,5},{5,6},{6,7},{7,0},{8,9},{9,10},{10,1... | collective-permute-start | bytes 294920 | tf_op jit(solution)/shard_map/ppermute | solution.py:53
  156.3 86.7 %reduce-scatter.12.cloned.1.call-start = ((), (), s32[]{:S(2)}) async-start(), calls=%async_computation.9 | async-start | bytes 884736
  156.9 2.0 copy-start.4
  211.0 107.6 %all-reduce.9.cloned.1.call-start = ((), (), s32[]{:S(2)}) async-start(), calls=%async_computation.6 | async-start | bytes 1572864 | tf_op jit(solution)/shard_map/psum | solution.py:10
  244.7 6.4 %collective-permute-start.7 = (f32[96,256]{0,1:T(8,128)S(1)}, f32[96,256]{0,1:T(8,128)S(1)}, u32[]{:S(2)}, u32[]{:S(2)}) collective-permute-start(f32[96,256]{0,1:T(8,128)S(1)} %get-tuple-element.15), channel_id=1, source_target_pairs={{0,1},{1,2},{2,3},{3,4},{4,5},{5,6},{6,7},{7,0},{8,9},{9,10},{10,1... | collective-permute-start | bytes 294920 | tf_op jit(solution)/shard_map/ppermute | solution.py:53
  244.8 6.5 %collective-permute-start.8 = (f32[96,256]{0,1:T(8,128)S(1)}, f32[96,256]{0,1:T(8,128)S(1)}, u32[]{:S(2)}, u32[]{:S(2)}) collective-permute-start(f32[96,256]{0,1:T(8,128)S(1)} %get-tuple-element.15), channel_id=1, source_target_pairs={{0,7},{1,0},{2,1},{3,2},{4,3},{5,4},{6,5},{7,6},{8,15},{9,8},{10,9... | collective-permute-start | bytes 294920 | tf_op jit(solution)/shard_map/ppermute | solution.py:58
  251.2 6.4 %collective-permute-start.9 = (f32[96,256]{0,1:T(8,128)S(1)}, f32[96,256]{0,1:T(8,128)S(1)}, u32[]{:S(2)}, u32[]{:S(2)}) collective-permute-start(f32[96,256]{0,1:T(8,128)S(1)} %collective-permute-done.7), channel_id=1, source_target_pairs={{0,1},{1,2},{2,3},{3,4},{4,5},{5,6},{6,7},{7,0},{8,9},{9,10},{10,1... | collective-permute-start | bytes 294920 | tf_op jit(solution)/shard_map/ppermute | solution.py:53
  251.4 6.4 %collective-permute-start.10 = (f32[96,256]{0,1:T(8,128)S(1)}, f32[96,256]{0,1:T(8,128)S(1)}, u32[]{:S(2)}, u32[]{:S(2)}) collective-permute-start(f32[96,256]{0,1:T(8,128)S(1)} %collective-permute-done.8), channel_id=1, source_target_pairs={{0,7},{1,0},{2,1},{3,2},{4,3},{5,4},{6,5},{7,6},{8,15},{9,8},{10,9... | collective-permute-start | bytes 294920 | tf_op jit(solution)/shard_map/ppermute | solution.py:58
  257.7 6.2 %collective-permute-start.11 = (f32[96,256]{0,1:T(8,128)S(1)}, f32[96,256]{0,1:T(8,128)S(1)}, u32[]{:S(2)}, u32[]{:S(2)}) collective-permute-start(f32[96,256]{0,1:T(8,128)S(1)} %collective-permute-done.9), channel_id=1, source_target_pairs={{0,1},{1,2},{2,3},{3,4},{4,5},{5,6},{6,7},{7,0},{8,9},{9,10},{10,1... | collective-permute-start | bytes 294920 | tf_op jit(solution)/shard_map/ppermute | solution.py:53
  257.9 6.2 %collective-permute-start.12 = (f32[96,256]{0,1:T(8,128)S(1)}, f32[96,256]{0,1:T(8,128)S(1)}, u32[]{:S(2)}, u32[]{:S(2)}) collective-permute-start(f32[96,256]{0,1:T(8,128)S(1)} %collective-permute-done.10), channel_id=1, source_target_pairs={{0,7},{1,0},{2,1},{3,2},{4,3},{5,4},{6,5},{7,6},{8,15},{9,8},{10,9... | collective-permute-start | bytes 294920 | tf_op jit(solution)/shard_map/ppermute | solution.py:58
  264.1 6.2 %collective-permute-start.13 = (f32[96,256]{0,1:T(8,128)S(1)}, f32[96,256]{0,1:T(8,128)S(1)}, u32[]{:S(2)}, u32[]{:S(2)}) collective-permute-start(f32[96,256]{0,1:T(8,128)S(1)} %collective-permute-done.11), channel_id=1, source_target_pairs={{0,1},{1,2},{2,3},{3,4},{4,5},{5,6},{6,7},{7,0},{8,9},{9,10},{10,1... | collective-permute-start | bytes 294920 | tf_op jit(solution)/shard_map/ppermute | solution.py:53
  271.4 86.6 %reduce-scatter.14.cloned.1.call-start = ((), (), s32[]{:S(2)}) async-start(), calls=%async_computation.10 | async-start | bytes 884736
  326.0 107.6 %all-reduce.11.cloned.1.call-start = ((), (), s32[]{:S(2)}) async-start(), calls=%async_computation.7 | async-start | bytes 1572864 | tf_op jit(solution)/shard_map/psum | solution.py:10
  359.8 6.4 %collective-permute-start.14 = (f32[96,256]{0,1:T(8,128)S(1)}, f32[96,256]{0,1:T(8,128)S(1)}, u32[]{:S(2)}, u32[]{:S(2)}) collective-permute-start(f32[96,256]{0,1:T(8,128)S(1)} %get-tuple-element.17), channel_id=1, source_target_pairs={{0,1},{1,2},{2,3},{3,4},{4,5},{5,6},{6,7},{7,0},{8,9},{9,10},{10,1... | collective-permute-start | bytes 294920 | tf_op jit(solution)/shard_map/ppermute | solution.py:53
  359.9 6.5 %collective-permute-start.15 = (f32[96,256]{0,1:T(8,128)S(1)}, f32[96,256]{0,1:T(8,128)S(1)}, u32[]{:S(2)}, u32[]{:S(2)}) collective-permute-start(f32[96,256]{0,1:T(8,128)S(1)} %get-tuple-element.17), channel_id=1, source_target_pairs={{0,7},{1,0},{2,1},{3,2},{4,3},{5,4},{6,5},{7,6},{8,15},{9,8},{10,9... | collective-permute-start | bytes 294920 | tf_op jit(solution)/shard_map/ppermute | solution.py:58
  366.3 6.4 %collective-permute-start.16 = (f32[96,256]{0,1:T(8,128)S(1)}, f32[96,256]{0,1:T(8,128)S(1)}, u32[]{:S(2)}, u32[]{:S(2)}) collective-permute-start(f32[96,256]{0,1:T(8,128)S(1)} %collective-permute-done.14), channel_id=1, source_target_pairs={{0,1},{1,2},{2,3},{3,4},{4,5},{5,6},{6,7},{7,0},{8,9},{9,10},{10,1... | collective-permute-start | bytes 294920 | tf_op jit(solution)/shard_map/ppermute | solution.py:53
  366.5 6.4 %collective-permute-start.17 = (f32[96,256]{0,1:T(8,128)S(1)}, f32[96,256]{0,1:T(8,128)S(1)}, u32[]{:S(2)}, u32[]{:S(2)}) collective-permute-start(f32[96,256]{0,1:T(8,128)S(1)} %collective-permute-done.15), channel_id=1, source_target_pairs={{0,7},{1,0},{2,1},{3,2},{4,3},{5,4},{6,5},{7,6},{8,15},{9,8},{10,9... | collective-permute-start | bytes 294920 | tf_op jit(solution)/shard_map/ppermute | solution.py:58
  372.8 6.2 %collective-permute-start.18 = (f32[96,256]{0,1:T(8,128)S(1)}, f32[96,256]{0,1:T(8,128)S(1)}, u32[]{:S(2)}, u32[]{:S(2)}) collective-permute-start(f32[96,256]{0,1:T(8,128)S(1)} %collective-permute-done.16), channel_id=1, source_target_pairs={{0,1},{1,2},{2,3},{3,4},{4,5},{5,6},{6,7},{7,0},{8,9},{9,10},{10,1... | collective-permute-start | bytes 294920 | tf_op jit(solution)/shard_map/ppermute | solution.py:53
  373.0 6.2 %collective-permute-start.19 = (f32[96,256]{0,1:T(8,128)S(1)}, f32[96,256]{0,1:T(8,128)S(1)}, u32[]{:S(2)}, u32[]{:S(2)}) collective-permute-start(f32[96,256]{0,1:T(8,128)S(1)} %collective-permute-done.17), channel_id=1, source_target_pairs={{0,7},{1,0},{2,1},{3,2},{4,3},{5,4},{6,5},{7,6},{8,15},{9,8},{10,9... | collective-permute-start | bytes 294920 | tf_op jit(solution)/shard_map/ppermute | solution.py:58
  379.2 6.2 %collective-permute-start.20 = (f32[96,256]{0,1:T(8,128)S(1)}, f32[96,256]{0,1:T(8,128)S(1)}, u32[]{:S(2)}, u32[]{:S(2)}) collective-permute-start(f32[96,256]{0,1:T(8,128)S(1)} %collective-permute-done.18), channel_id=1, source_target_pairs={{0,1},{1,2},{2,3},{3,4},{4,5},{5,6},{6,7},{7,0},{8,9},{9,10},{10,1... | collective-permute-start | bytes 294920 | tf_op jit(solution)/shard_map/ppermute | solution.py:53
  386.5 48.2 %copy-start.2 = (f32[768,256]{1,0:T(8,128)S(1)}, f32[768,256]{1,0:T(8,128)}, u32[]{:S(2)}) copy-start(f32[768,256]{1,0:T(8,128)} %get-tuple-element.9) | copy-start | bytes 2359300
  (2 other events, 2.8 us)
Sparse Core Ops, SparseCore 0:
  9.6 25.4 all-gather.1
  38.8 53.9 all-reduce.4
  96.0 31.8 reduce-scatter.9
  156.4 47.0 all-reduce.6
  211.1 31.8 reduce-scatter.11
  271.5 46.9 all-reduce.8
  326.1 31.8 reduce-scatter.13
  386.6 46.9 all-reduce.10
